TPU v7x, 32 devices: a whole 2x2x4 slice. The times are simulated.
32 devices in a mesh: facet: 8 (over y, x, core), col: 4 (over z).
Axes of the slice: x: 2, y: 2, z: 4, core: 2. Of those that a mesh axis runs over, the one named last changes fastest.
Arguments:
- facets: float32 [2, 8, 24, 2, 4096], P(None, 'facet', None, None, 'col'), may hold values from -6 to 6
- facet_x: int32 [8], P('facet'), may hold values from 0 to 32767
- facet_y: int32 [2], replicated, may hold values from 0 to 32767
- col_u: int32 [8], replicated, may hold values from 0 to 32767
- slot_col: int32 [4, 8], P('col'), may hold values from 0 to 1
- slot_v: int32 [4, 8], P('col'), may hold values from 0 to 32767
Outputs:
- subgrids: float32 [4, 8, 512, 1024], P('col', 'facet')
Inputs may be any that keep to these rules, and one draw needn't show every extreme that they name: `col_u`: offset in the image. `slot_col`: the subgrid's column is owner * 2 + this value. `slot_v`: offset in the image.
All inputs are finite; a program needn't handle non-finite values.
Results may differ from a plain program's by a relative error of at most 0.0003.
Values sent between devices are 32-bit elements; how exact they have to be, the bound alone decides.
A program may use at most 128 MiB of HBM per device.

v0:
```python
import functools
import math

import jax
import jax.numpy as jnp
from jax import lax
from jax.experimental import pallas as pl
from jax.experimental.pallas import tpu as pltpu
from jax.sharding import PartitionSpec as P

SG = 512
HALF = SG // 2
COLS_DEV = 2
F32 = jnp.float32
BF16 = jnp.bfloat16
I32 = jnp.int32
MESH = pl.DeviceIdType.MESH


def turn(m, mod):
    bits = mod.bit_length() - 1
    m = m & (mod - 1)
    quad = lax.shift_right_logical(m + (mod >> 3), jnp.int32(bits - 2))
    rest = m - lax.shift_left(quad, jnp.int32(bits - 2))
    t = rest.astype(F32) * F32(2.0 * math.pi / mod)
    t2 = t * t
    sine = t + t * t2 * (F32(-1 / 6) + t2 * (F32(1 / 120) + t2 * F32(-1 / 5040)))
    cosine = F32(1.0) + t2 * (
        F32(-0.5) + t2 * (F32(1 / 24) + t2 * (F32(-1 / 720) + t2 * F32(1 / 40320)))
    )
    odd = (quad & 1) == 1
    c = jnp.where(odd, sine, cosine)
    s = jnp.where(odd, cosine, sine)
    c = jnp.where(((quad + 1) & 2) == 2, -c, c)
    s = jnp.where((quad & 2) == 2, -s, s)
    return c, s


def split(value):
    high = value.astype(BF16)
    return high, (value - high.astype(F32)).astype(BF16)


def mm(a, b):
    return jnp.dot(a, b, preferred_element_type=F32)


def partner(index, count, step):
    if count & (count - 1):
        return lax.rem(index + step, count)
    bit = 1
    while bit < count:
        if step & bit:
            index = index + bit - 2 * bit * lax.rem(lax.div(index, bit), 2)
        bit *= 2
    return index


def gather_kernel(
    nf, nc, img, band, cuts, hpad,
    fx_ref, fy_hbm, u_hbm, sc_hbm, sv_hbm, facets_ref,
    h_ref, e_ref,
    cells, fxs, fxall, table, premod, phase, zbuf, part, zrecv, gsend, gat,
    fy_ref, u_ref, sc_ref, sv_ref,
    s_a2a, r_a2a, s_fx, r_fx, s_z, r_z, s_g, r_g, l_sem, i_sem,
):
    f = lax.axis_index("facet")
    c = lax.axis_index("col")
    rows = facets_ref.shape[0]
    rpd = rows // nf
    width = facets_ref.shape[-1]
    mod = 2 * img
    ncol = COLS_DEV * nc
    depth = len(cuts) * nf * hpad

    fxs[...] = jnp.full(fxs.shape, fx_ref[0], I32)
    numbers = []
    for i, (src, dst) in enumerate((
        (fy_hbm, fy_ref), (u_hbm, u_ref), (sc_hbm, sc_ref), (sv_hbm, sv_ref)
    )):
        copy = pltpu.make_async_copy(src, dst, i_sem.at[i])
        copy.start()
        numbers.append(copy)
    barrier = pltpu.get_barrier_semaphore()
    for d in range(1, nf):
        pl.semaphore_signal(barrier, inc=1, device_id=(partner(f, nf, d), c), device_id_type=MESH)
    for d in range(1, nc):
        pl.semaphore_signal(barrier, inc=1, device_id=(f, partner(c, nc, d)), device_id_type=MESH)

    pl.semaphore_wait(barrier, nf + nc - 2)

    small = []
    sends = []
    for d in range(1, nf):
        copy = pltpu.make_async_remote_copy(
            src_ref=fxs, dst_ref=fxall.at[f],
            send_sem=s_fx.at[d], recv_sem=r_fx.at[d],
            device_id=(partner(f, nf, d), c), device_id_type=MESH,
        )
        copy.start()
        small.append(copy)
    copy = pltpu.make_async_copy(fxs, fxall.at[f], l_sem.at[len(cuts)])
    copy.start()
    small.append(copy)
    for n, (y0, ny) in enumerate(cuts):
        group = []
        for d in range(1, nf):
            peer = partner(f, nf, d)
            copy = pltpu.make_async_remote_copy(
                src_ref=facets_ref.at[pl.ds(peer * rpd + y0, ny)],
                dst_ref=cells.at[pl.ds(y0, ny), :, f],
                send_sem=s_a2a.at[n, d], recv_sem=r_a2a.at[n, d],
                device_id=(peer, c), device_id_type=MESH,
            )
            copy.start()
            group.append(copy)
        copy = pltpu.make_async_copy(
            facets_ref.at[pl.ds(f * rpd + y0, ny)], cells.at[pl.ds(y0, ny), :, f], l_sem.at[n]
        )
        copy.start()
        group.append(copy)
        sends.append(group)

    for copy in numbers:
        copy.wait()
    start = c * width
    xs = lax.broadcasted_iota(I32, (ncol, width), 1) + start
    row = lax.broadcasted_iota(I32, (ncol, width), 0)
    uv = jnp.zeros((ncol, width), I32)
    for i in range(ncol):
        uv = jnp.where(row == i, u_ref[i], uv)
    pc, ps = turn((2 * uv + (SG - 1)) * xs, mod)
    premod[0] = pc
    premod[1] = ps
    h_ref[...] = jnp.zeros_like(h_ref)
    block = 64

    def table_step(i, carry):
        first = pl.multiple_of(i * block, block)
        x = lax.broadcasted_iota(I32, (block, HALF), 0) + (start + first)
        j = lax.broadcasted_iota(I32, (block, HALF), 1)
        cosine, sine = turn((2 * j + 1) * x, mod)
        ch, cl = split(cosine)
        sh, sl = split(sine)
        table[0, pl.ds(first, block), pl.ds(0, HALF)] = ch
        table[0, pl.ds(first, block), pl.ds(HALF, HALF)] = sh
        table[1, pl.ds(first, block), pl.ds(0, HALF)] = cl
        table[1, pl.ds(first, block), pl.ds(HALF, HALF)] = sl
        return carry

    lax.fori_loop(0, width // block, table_step, 0)

    for copy in small:
        copy.wait()
    fx = fxall[:, 0, :]
    fx = jnp.concatenate([fx] * (SG // fx.shape[-1]), axis=1)
    lane = lax.broadcasted_iota(I32, (nf, SG), 1)
    a = jnp.where(lane < HALF, HALF + lane, SG - 1 - lane)

    def phase_step(i, carry):
        wc, ws = turn(2 * (a + u_ref[i]) * fx, mod)
        phase[0, i] = wc
        phase[1, i] = ws
        return carry

    lax.fori_loop(0, ncol, phase_step, 0)

    def transform(n):
        y0, ny = cuts[n]
        size = ny * nf
        for d in list(range(nc - 1, 0, -1)) + [0]:
            owner = partner(c, nc, d)
            for s in range(COLS_DEV):
                col = owner * COLS_DEV + s
                cosine = premod[0, pl.ds(col, 1), :].reshape(1, 1, width)
                sine = premod[1, pl.ds(col, 1), :].reshape(1, 1, width)
                re = cells[pl.ds(y0, ny), 0]
                im = cells[pl.ds(y0, ny), 1]
                zr = (re * cosine + im * sine).reshape(size, width)
                zi = (im * cosine - re * sine).reshape(size, width)
                for m, z in enumerate((zr, zi)):
                    hi, lo = split(z)
                    at = (s * 2 + m) * size
                    zbuf[0, pl.ds(at, size), :] = hi
                    zbuf[1, pl.ds(at, size), :] = lo
            every = pl.ds(0, 2 * COLS_DEV * size)
            high = zbuf[0, every, :]
            prod = mm(high, table[0]) + mm(zbuf[1, every, :], table[0]) + mm(high, table[1])
            for s in range(COLS_DEV):
                col = owner * COLS_DEV + s
                at = s * 2 * size
                fr = prod[at:at + size]
                fi = prod[at + size:at + 2 * size]
                rc, rs = fr[:, :HALF], fr[:, HALF:]
                ic, is_ = fi[:, :HALF], fi[:, HALF:]
                hr = jnp.concatenate([rc + is_, rc - is_], axis=1).reshape(ny, nf, SG)
                hm = jnp.concatenate([ic - rs, ic + rs], axis=1).reshape(ny, nf, SG)
                wc = phase[0, col]
                ws = phase[1, col]
                part[n, d, pl.ds(s * ny, ny), pl.ds(0, SG)] = jnp.sum(hr * wc + hm * ws, axis=1)
                part[n, d, pl.ds(s * ny, ny), pl.ds(SG, SG)] = jnp.sum(hm * wc - hr * ws, axis=1)
            if d:
                copy = pltpu.make_async_remote_copy(
                    src_ref=part.at[n, d], dst_ref=zrecv.at[n, d],
                    send_sem=s_z.at[n, d], recv_sem=r_z.at[n, d],
                    device_id=(f, owner), device_id_type=MESH,
                )
                copy.start()
                zcopies[n].append((d, copy))

    scale = 1.0 / math.sqrt(1.0 * rows * width * nc * nf)

    def v_step(i, carry):
        first = pl.multiple_of(i * block, block)
        b = lax.broadcasted_iota(I32, (block, depth), 0) + first
        q = lax.broadcasted_iota(I32, (block, depth), 1)
        inner = lax.rem(q, hpad)
        peer = lax.rem(lax.div(q, hpad), nf)
        piece = lax.div(q, hpad * nf)
        g = peer * rpd + inner
        for n, (y0, ny) in enumerate(cuts):
            g = jnp.where(piece == n, g + y0, g)
        cell = jnp.where(g < band, fy_ref[0] + g, fy_ref[1] + g - band)
        cosine, sine = turn(2 * (sv_ref[f] + b) * cell, mod)
        wide = jnp.concatenate([cosine, sine], axis=1) * F32(scale)
        hi, lo = split(wide)
        e_ref[pl.ds(first, block), pl.ds(0, 2 * depth)] = hi
        e_ref[pl.ds(first, block), pl.ds(2 * depth, 2 * depth)] = lo
        e_ref[pl.ds(first, block), pl.ds(4 * depth, 2 * depth)] = hi
        return carry

    zcopies = [[] for _ in cuts]
    for n in range(len(cuts)):
        for copy in sends[n]:
            copy.wait()
        transform(n)
    lax.fori_loop(0, SG // block, v_step, 0)

    flip = lax.broadcasted_iota(I32, (HALF, HALF), 0) + lax.broadcasted_iota(I32, (HALF, HALF), 1)
    flip = jnp.where(flip == HALF - 1, F32(1.0), F32(0.0)).astype(BF16)
    gcopies = []
    for n, (y0, ny) in enumerate(cuts):
        acc = part[n, 0]
        for d, copy in zcopies[n]:
            copy.wait()
            acc = acc + zrecv[n, d]
        pieces = []
        for m in range(2):
            hi, lo = split(acc[:, m * SG + HALF:(m + 1) * SG])
            pieces += [mm(hi, flip) + mm(lo, flip), acc[:, m * SG:m * SG + HALF]]
        total = jnp.concatenate(pieces, axis=1)
        options = [total[s * ny:(s + 1) * ny] for s in range(COLS_DEV)]
        group = []
        for d in range(1, nf):
            peer = partner(f, nf, d)
            chosen = options[0]
            for s in range(1, COLS_DEV):
                chosen = jnp.where(sc_ref[peer] == s, options[s], chosen)
            gsend[n, d, pl.ds(0, ny), :] = chosen
            copy = pltpu.make_async_remote_copy(
                src_ref=gsend.at[n, d], dst_ref=gat.at[n, f],
                send_sem=s_g.at[n, d], recv_sem=r_g.at[n, d],
                device_id=(peer, c), device_id_type=MESH,
            )
            copy.start()
            gcopies.append(copy)
        chosen = options[0]
        for s in range(1, COLS_DEV):
            chosen = jnp.where(sc_ref[f] == s, options[s], chosen)
        gat[n, f, pl.ds(0, ny), :] = chosen
    for copy in gcopies:
        copy.wait()
    for n, (y0, ny) in enumerate(cuts):
        for j in range(nf):
            h_ref[pl.ds((n * nf + j) * hpad, ny), :] = gat[n, j, pl.ds(0, ny), :]


def v_kernel(h_ref, e_ref, out_ref, rhs):
    @pl.when(pl.program_id(0) == 0)
    def _():
        k = h_ref.shape[0]
        hi, lo = split(h_ref[...])
        for n, h in enumerate((hi, hi, lo)):
            rhs[pl.ds(2 * n * k, k), :] = h
            rhs[pl.ds((2 * n + 1) * k, k), pl.ds(0, SG)] = h[:, SG:]
            rhs[pl.ds((2 * n + 1) * k, k), pl.ds(SG, SG)] = -h[:, :SG]

    out_ref[...] = mm(e_ref[...], rhs[...])


def per_device(nf, nc, facets, facet_x, facet_y, col_u, slot_col, slot_v):
    width = facets.shape[-1]
    band = facets.shape[2]
    img = width * nc * nf
    rows = facets.shape[0] * band
    rpd = rows // nf
    ncol = COLS_DEV * nc
    cuts = ((0, rpd // 2), (rpd // 2, rpd - rpd // 2))
    most = rpd - rpd // 2
    hpad = 1 << (most - 1).bit_length()
    depth = len(cuts) * nf * hpad
    pieces = len(cuts)
    vm = pl.BlockSpec(memory_space=pltpu.VMEM)
    dma = pltpu.SemaphoreType.DMA
    h, e = pl.pallas_call(
        functools.partial(gather_kernel, nf, nc, img, band, cuts, hpad),
        out_shape=(
            jax.ShapeDtypeStruct((depth, 2 * SG), F32),
            jax.ShapeDtypeStruct((SG, 6 * depth), BF16),
        ),
        in_specs=[pl.BlockSpec(memory_space=pltpu.SMEM)] + [pl.BlockSpec(memory_space=pltpu.HBM)] * 5,
        out_specs=(vm, vm),
        scratch_shapes=[
            pltpu.VMEM((rpd, 2, nf, width), F32),
            pltpu.VMEM((8, 128), I32),
            pltpu.VMEM((nf, 8, 128), I32),
            pltpu.VMEM((2, width, SG), BF16),
            pltpu.VMEM((2, ncol, width), F32),
            pltpu.VMEM((2, ncol, nf, SG), F32),
            pltpu.VMEM((2, 2 * COLS_DEV * most * nf, width), BF16),
            pltpu.VMEM((pieces, nc, COLS_DEV * most, 2 * SG), F32),
            pltpu.VMEM((pieces, nc, COLS_DEV * most, 2 * SG), F32),
            pltpu.VMEM((pieces, nf, most, 2 * SG), F32),
            pltpu.VMEM((pieces, nf, most, 2 * SG), F32),
            pltpu.SMEM((2,), I32), pltpu.SMEM((ncol,), I32),
            pltpu.SMEM((nf,), I32), pltpu.SMEM((nf,), I32),
            dma((pieces, nf)), dma((pieces, nf)), dma((nf,)), dma((nf,)),
            dma((pieces, nc)), dma((pieces, nc)), dma((pieces, nf)), dma((pieces, nf)),
            dma((pieces + 1,)), dma((4,)),
        ],
        compiler_params=pltpu.CompilerParams(
            collective_id=0, has_side_effects=True, vmem_limit_bytes=24 << 20
        ),
        name="gather_columns",
    )(facet_x, *(
        pltpu.with_memory_space_constraint(z, pltpu.HBM)
        for z in (facet_y, col_u, slot_col[0], slot_v[0], facets.reshape(rows, 2, width))
    ))
    tile = 128
    out = pl.pallas_call(
        v_kernel,
        grid=(SG // tile,),
        out_shape=jax.ShapeDtypeStruct((SG, 2 * SG), F32),
        in_specs=[
            pl.BlockSpec((depth, 2 * SG), lambda i: (0, 0)),
            pl.BlockSpec((tile, 6 * depth), lambda i: (i, 0)),
        ],
        out_specs=pl.BlockSpec((tile, 2 * SG), lambda i: (i, 0)),
        scratch_shapes=[pltpu.VMEM((6 * depth, 2 * SG), BF16)],
        compiler_params=pltpu.CompilerParams(vmem_limit_bytes=24 << 20),
        name="v_transform",
    )(h, e)
    return out[None, None]


def solution(mesh):
    placed = (
        P(None, "facet", None, None, "col"),
        P("facet"),
        P(),
        P(),
        P("col", None),
        P("col", None),
    )
    return jax.shard_map(
        functools.partial(per_device, mesh.shape["facet"], mesh.shape["col"]),
        mesh=mesh,
        in_specs=placed,
        out_specs=P("col", "facet", None, None),
        check_vma=False,
    )
```

profile of v0, /device:TPU:0, one launch (start us, length us, event | category | flops | bytes accessed | tf_op | source)
XLA Modules:
  0.0 27.1 jit_solution(10872432005364684699)
XLA Ops:
  0.7 23.8 %gather_columns.1 = (f32[64,1024]{1,0:T(8,128)S(1)}, bf16[512,384]{1,0:T(8,128)(2,1)S(1)}) custom-call(s32[1]{0:T(128)S(6)} %copy.7.fx_ref, s32[2]{0:T(128)} %fy_hbm.1, s32[8]{0:T(128)} %u_hbm.1, s32[8]{0:T(128)} %bitcast.5, s32[8]{0:T(128)} %bitcast.6, f32[48,2,1024]{2,1,0:T(2,128)} %bitcast.4), custom_call_target="tpu_custom_call" | custom-call | tf_op jit(solution)/shard_map/gather_columns/pallas_call | solution.py:305
  24.4 2.6 %v_transform.1 = f32[512,1024]{1,0:T(8,128)} custom-call(f32[64,1024]{1,0:T(8,128)S(1)} %get-tuple-element.7.h_ref, bf16[512,384]{1,0:T(8,128)(2,1)S(1)} %get-tuple-element.8.e_ref), custom_call_target="tpu_custom_call" | custom-call | tf_op jit(solution)/shard_map/v_transform/pallas_call | solution.py:340
where the time goes:
time: 27.2 us; the launch traced here: 27.1 us
  Pallas kernels  26.4 us (97%)
  between operations  0.66 us (2%)
    pallas_call x1, Pallas kernels, per_device(): pl.pallas_call(functools.partial(gather_kernel, nf, nc, img, band, cuts,...  23.8 us
    pallas_call x1, Pallas kernels, per_device(): pl.pallas_call(v_kernel, grid=(SG // tile,), out_shape=jax.ShapeDtypeStru...  2.64 us

commit v1 on v0

v1 whole, which is shorter than its diff:
```python
import functools
import math

import jax
import jax.numpy as jnp
from jax import lax
from jax.experimental import pallas as pl
from jax.experimental.pallas import tpu as pltpu
from jax.sharding import PartitionSpec as P

SG = 512
HALF = SG // 2
COLS_DEV = 2
LANES = 128
F32 = jnp.float32
BF16 = jnp.bfloat16
I32 = jnp.int32
MESH = pl.DeviceIdType.MESH


def turn(m, mod):
    bits = mod.bit_length() - 1
    m = m & (mod - 1)
    quad = lax.shift_right_logical(m + (mod >> 3), jnp.int32(bits - 2))
    rest = m - lax.shift_left(quad, jnp.int32(bits - 2))
    t = rest.astype(F32) * F32(2.0 * math.pi / mod)
    t2 = t * t
    sine = t + t * t2 * (F32(-1 / 6) + t2 * (F32(1 / 120) + t2 * F32(-1 / 5040)))
    cosine = F32(1.0) + t2 * (
        F32(-0.5) + t2 * (F32(1 / 24) + t2 * (F32(-1 / 720) + t2 * F32(1 / 40320)))
    )
    odd = (quad & 1) == 1
    c = jnp.where(odd, sine, cosine)
    s = jnp.where(odd, cosine, sine)
    c = jnp.where(((quad + 1) & 2) == 2, -c, c)
    s = jnp.where((quad & 2) == 2, -s, s)
    return c, s


def split(value):
    high = value.astype(BF16)
    return high, (value - high.astype(F32)).astype(BF16)


def mm(a, b):
    return jnp.dot(a, b, preferred_element_type=F32)


def partner(index, count, step):
    if count & (count - 1):
        return lax.rem(index + step, count)
    bit = 1
    while bit < count:
        if step & bit:
            index = index + bit - 2 * bit * lax.rem(lax.div(index, bit), 2)
        bit *= 2
    return index


def mirrored(pieces):
    rows = pieces[0].shape[0]
    lane = LANES - 1 - lax.broadcasted_iota(I32, (rows, LANES), 1)
    return [jnp.take_along_axis(p, lane, axis=1) for p in reversed(pieces)]


def tiles(ref_row, first, count):
    return [ref_row[:, first + i * LANES:first + (i + 1) * LANES] for i in range(count)]


def stack(h_ref, rhs):
    k = h_ref.shape[0]
    hi, lo = split(h_ref[...])
    for n, h in enumerate((hi, hi, lo)):
        rhs[pl.ds(2 * n * k, k), :] = h
        rhs[pl.ds((2 * n + 1) * k, k), pl.ds(0, SG)] = h[:, SG:]
        rhs[pl.ds((2 * n + 1) * k, k), pl.ds(SG, SG)] = -h[:, :SG]
    if rhs.shape[0] > 6 * k:
        rhs[pl.ds(6 * k, rhs.shape[0] - 6 * k), :] = jnp.zeros((rhs.shape[0] - 6 * k, 2 * SG), BF16)


def lanes_of(rows):
    return -(-6 * rows // LANES) * LANES


def gather_kernel(
    nf, nc, img, band,
    fx_hbm, fy_hbm, u_hbm, sc_hbm, sv_hbm, facets_ref,
    acc_ref, h_ref, e_ref,
    hbuf, e1, rhs, cells, fxs, fxall, table, premod, phase, eo, zbuf, part, zrecv, gsend,
    fx_ref, fy_ref, u_ref, sc_ref, sv_ref,
    s_a2a, r_a2a, x_sem, s_z, r_z, g_sem, i_sem, z_sem,
):
    f = lax.axis_index("facet")
    c = lax.axis_index("col")
    rows = facets_ref.shape[0]
    rpd = rows // nf
    width = facets_ref.shape[-1]
    half = width // 2
    ncol = COLS_DEV * nc
    depth = rpd * nf
    tail = h_ref.shape[0]

    numbers = []
    for i, (src, dst) in enumerate((
        (fx_hbm, fx_ref), (fy_hbm, fy_ref), (u_hbm, u_ref), (sc_hbm, sc_ref), (sv_hbm, sv_ref)
    )):
        copy = pltpu.make_async_copy(src, dst, i_sem.at[i])
        copy.start()
        numbers.append(copy)
    barrier = pltpu.get_barrier_semaphore()
    for d in range(1, nf):
        pl.semaphore_signal(barrier, inc=1, device_id=(partner(f, nf, d), c), device_id_type=MESH)

    def tell_above(z, carry):
        pl.semaphore_signal(barrier, inc=1, device_id=(f, z), device_id_type=MESH)
        return carry

    lax.fori_loop(c + 1, nc, tell_above, 0)
    pl.semaphore_wait(barrier, nf - 1 + c)

    def done(ref, sem):
        pltpu.make_async_copy(ref, ref, sem).wait()

    numbers[0].wait()
    fxs[...] = jnp.full(fxs.shape, fx_ref[0], I32)
    for d in range(1, nf):
        pltpu.make_async_remote_copy(
            src_ref=fxs, dst_ref=fxall.at[f], send_sem=x_sem.at[0], recv_sem=x_sem.at[1],
            device_id=(partner(f, nf, d), c), device_id_type=MESH,
        ).start()
    pltpu.make_async_copy(fxs, fxall.at[f], x_sem.at[1]).start()
    for y in range(rpd):
        for d in range(1, nf):
            peer = partner(f, nf, d)
            pltpu.make_async_remote_copy(
                src_ref=facets_ref.at[peer * rpd + y], dst_ref=cells.at[y, :, f],
                send_sem=s_a2a, recv_sem=r_a2a.at[y],
                device_id=(peer, c), device_id_type=MESH,
            ).start()
        pltpu.make_async_copy(facets_ref.at[f * rpd + y], cells.at[y, :, f], r_a2a.at[y]).start()

    def tell_below(z, carry):
        pl.semaphore_signal(z_sem, inc=1, device_id=(f, z), device_id_type=MESH)
        return carry

    lax.fori_loop(0, c, tell_below, 0)
    for copy in numbers[1:]:
        copy.wait()

    uv = jnp.zeros((ncol, half), I32)
    row = lax.broadcasted_iota(I32, (ncol, half), 0)
    for i in range(ncol):
        uv = jnp.where(row == i, u_ref[i], uv)
    x2 = 2 * lax.broadcasted_iota(I32, (ncol, half), 1) + 1
    pc, ps = turn((2 * uv + (SG - 1)) * x2, 4 * img)
    premod[0] = pc
    premod[1] = ps
    block = 64

    def table_step(i, carry):
        first = pl.multiple_of(i * block, block)
        x = 2 * (lax.broadcasted_iota(I32, (block, HALF), 0) + first) + 1
        j = 2 * lax.broadcasted_iota(I32, (block, HALF), 1) + 1
        for n, value in enumerate(turn(j * x, 4 * img)):
            hi, lo = split(value)
            table[n, 0, pl.ds(first, block), :] = hi
            table[n, 1, pl.ds(first, block), :] = lo
        return carry

    lax.fori_loop(0, half // block, table_step, 0)

    scale = 1.0 / math.sqrt(1.0 * rows * width * nc * nf)
    for target, first_row, count in ((e1, 0, depth - tail), (e_ref, depth - tail, tail)):
        lanes = target.shape[1]
        q = lax.broadcasted_iota(I32, (1, lanes), 1)
        term = lax.div(q, 2 * count)
        inner = q - term * (2 * count)
        quarter = jnp.where(inner < count, 0, img // 4)
        at = jnp.where(inner < count, inner, inner - count) + first_row
        g = lax.rem(at, nf) * rpd + lax.div(at, nf)
        cell = jnp.where(g < band, fy_ref[0] + g, fy_ref[1] + g - band)
        cell, quarter, term = (jnp.broadcast_to(z, (block, lanes)) for z in (cell, quarter, term))

        def v_step(i, carry):
            first = pl.multiple_of(i * block, block)
            b = lax.broadcasted_iota(I32, (block, lanes), 0) + first
            value = turn((sv_ref[f] + b) * cell - quarter, img)[0] * F32(scale)
            high = value.astype(BF16).astype(F32)
            value = jnp.where(term == 1, value - high, high)
            target[pl.ds(first, block), :] = jnp.where(term < 3, value, F32(0.0)).astype(BF16)
            return carry

        lax.fori_loop(0, SG // block, v_step, 0)

    done(fxall, x_sem.at[1])
    lane = lax.broadcasted_iota(I32, (ncol, SG), 1)
    uv = jnp.zeros((ncol, SG), I32)
    row = lax.broadcasted_iota(I32, (ncol, SG), 0)
    for i in range(ncol):
        uv = jnp.where(row == i, u_ref[i], uv)
    ua = uv + jnp.where(lane < HALF, HALF + lane, SG - 1 - lane)
    shift = 2 * c * width + width - 1

    def phase_step(k, carry):
        fx = jnp.broadcast_to(fxall[k], (ncol, LANES))
        fx = jnp.concatenate([2 * fx + shift] * (SG // LANES), axis=1)
        wc, ws = turn(ua * fx, 2 * img)
        phase[0, k] = wc
        phase[1, k] = ws
        return carry

    lax.fori_loop(0, nf, phase_step, 0)
    nt = half // LANES

    def row_step(y, carry):
        done(cells.at[y], r_a2a.at[y])
        for m in range(2):
            value = cells[y, m]
            upper = tiles(value, half, nt)
            lower = mirrored(tiles(value, 0, nt))
            for j in range(nt):
                eo[m, :, j * LANES:(j + 1) * LANES] = upper[j] + lower[j]
                eo[2 + m, :, j * LANES:(j + 1) * LANES] = upper[j] - lower[j]
        cosine = premod[0]
        sine = premod[1]
        size = 2 * ncol * nf
        for k in range(nf):
            er, ei, dr, di = (
                jnp.broadcast_to(eo[m, pl.ds(k, 1), :], (ncol, half)) for m in range(4)
            )
            even = jnp.concatenate([er * cosine + di * sine, ei * cosine - dr * sine], axis=0)
            odd = jnp.concatenate([dr * cosine + ei * sine, di * cosine - er * sine], axis=0)
            at = pl.ds(k * 2 * ncol, 2 * ncol)
            for n, value in enumerate((even, odd)):
                hi, lo = split(value)
                zbuf[n, at, :] = hi
                zbuf[n, pl.ds(size + k * 2 * ncol, 2 * ncol), :] = lo
        prod = []
        for n in range(2):
            both = mm(zbuf[n], table[n, 0])
            prod.append(both[:size] + both[size:] + mm(zbuf[n, :size, :], table[n, 1]))
        re = jnp.zeros((ncol, SG), F32)
        im = jnp.zeros((ncol, SG), F32)
        for k in range(nf):
            at = 2 * k * ncol
            rc, ic = prod[0][at:at + ncol], prod[0][at + ncol:at + 2 * ncol]
            rs, is_ = prod[1][at:at + ncol], prod[1][at + ncol:at + 2 * ncol]
            hr = jnp.concatenate([rc + is_, rc - is_], axis=1)
            hm = jnp.concatenate([ic - rs, ic + rs], axis=1)
            wc = phase[0, k]
            ws = phase[1, k]
            re = re + (hr * wc + hm * ws)
            im = im + (hm * wc - hr * ws)
        part[y, :, 0:SG] = re
        part[y, :, SG:2 * SG] = im

        @pl.when((y == 0) & (c < nc - 1))
        def _():
            pl.semaphore_wait(z_sem, nc - 1 - c)

        for d in range(nc - 1):
            owner = jnp.where(d < c, d, d + 1)
            pltpu.make_async_remote_copy(
                src_ref=part.at[y, pl.ds(owner * COLS_DEV, COLS_DEV)], dst_ref=zrecv.at[y, c],
                send_sem=s_z, recv_sem=r_z.at[y],
                device_id=(f, owner), device_id_type=MESH,
            ).start()
        pltpu.make_async_copy(
            part.at[y, pl.ds(c * COLS_DEV, COLS_DEV)], zrecv.at[y, c], r_z.at[y]
        ).start()
        return carry

    lax.fori_loop(0, rpd, row_step, 0)

    slot = lax.broadcasted_iota(I32, (nf, SG), 0)
    which = jnp.zeros((nf, SG), I32)
    for d in range(nf):
        which = jnp.where(slot == d, sc_ref[partner(f, nf, d)], which)

    nh = HALF // LANES

    def sum_step(target, y0, sem, y, carry):
        done(zrecv.at[y], r_z.at[y])
        acc = zrecv[y, 0]
        for d in range(1, nc):
            acc = acc + zrecv[y, d]
        for m in range(2):
            value = acc[:, m * SG:(m + 1) * SG]
            chosen = jnp.broadcast_to(value[0:1], (nf, SG))
            for s in range(1, COLS_DEV):
                chosen = jnp.where(which == s, jnp.broadcast_to(value[s:s + 1], (nf, SG)), chosen)
            upper = tiles(chosen, 0, nh)
            lower = mirrored(tiles(chosen, HALF, nh))
            gsend[y, :, m * SG:(m + 1) * SG] = jnp.concatenate(lower + upper, axis=1)
        for d in range(1, nf):
            pltpu.make_async_remote_copy(
                src_ref=gsend.at[y, d], dst_ref=target.at[(y - y0) * nf + f],
                send_sem=g_sem.at[0], recv_sem=sem,
                device_id=(partner(f, nf, d), c), device_id_type=MESH,
            ).start()
        pltpu.make_async_copy(gsend.at[y, 0], target.at[(y - y0) * nf + f], sem).start()
        return carry

    cut = rpd - tail // nf
    lax.fori_loop(0, cut, functools.partial(sum_step, hbuf, 0, g_sem.at[1]), 0)
    lax.fori_loop(cut, rpd, functools.partial(sum_step, h_ref, cut, g_sem.at[2]), 0)
    done(hbuf, g_sem.at[1])
    stack(hbuf, rhs)
    acc_ref[...] = mm(e1[...], rhs[...])
    done(h_ref, g_sem.at[2])
    done(fxall.at[pl.ds(0, nf - 1)], x_sem.at[0])
    done(facets_ref.at[pl.ds(0, (nf - 1) * rpd)], s_a2a)
    done(zrecv.at[:, pl.ds(1, nc - 1)], s_z)
    done(facets_ref.at[pl.ds(0, (nf - 1) * rpd * SG // width)], g_sem.at[0])


def v_kernel(acc_ref, h_ref, e_ref, out_ref, rhs, buf, sem):
    stack(h_ref, rhs)
    copies = []
    chunk = 2 * LANES
    for i in range(2 * SG // chunk):
        at = pl.ds(i * chunk, chunk)
        buf[:, at] = acc_ref[:, at] + mm(e_ref[...], rhs[:, at])
        copies.append(pltpu.make_async_copy(buf.at[:, at], out_ref.at[:, at], sem.at[i]))
        copies[-1].start()
    for copy in copies:
        copy.wait()


def per_device(nf, nc, facets, facet_x, facet_y, col_u, slot_col, slot_v):
    width = facets.shape[-1]
    band = facets.shape[2]
    img = width * nc * nf
    rows = facets.shape[0] * band
    rpd = rows // nf
    ncol = COLS_DEV * nc
    depth = rpd * nf
    half = width // 2
    tail = (rpd - 2 * rpd // 3) * nf
    vm = pl.BlockSpec(memory_space=pltpu.VMEM)
    dma = pltpu.SemaphoreType.DMA
    acc, h, e = pl.pallas_call(
        functools.partial(gather_kernel, nf, nc, img, band),
        out_shape=(
            jax.ShapeDtypeStruct((SG, 2 * SG), F32),
            jax.ShapeDtypeStruct((tail, 2 * SG), F32),
            jax.ShapeDtypeStruct((SG, lanes_of(tail)), BF16),
        ),
        in_specs=[pl.BlockSpec(memory_space=pl.ANY)] + [pl.BlockSpec(memory_space=pltpu.HBM)] * 5,
        out_specs=(vm, vm, vm),
        scratch_shapes=[
            pltpu.VMEM((depth - tail, 2 * SG), F32),
            pltpu.VMEM((SG, lanes_of(depth - tail)), BF16),
            pltpu.VMEM((lanes_of(depth - tail), 2 * SG), BF16),
            pltpu.VMEM((rpd, 2, nf, width), F32),
            pltpu.VMEM((1, LANES), I32),
            pltpu.VMEM((nf, 1, LANES), I32),
            pltpu.VMEM((2, 2, half, HALF), BF16),
            pltpu.VMEM((2, ncol, half), F32),
            pltpu.VMEM((2, nf, ncol, SG), F32),
            pltpu.VMEM((4, nf, half), F32),
            pltpu.VMEM((2, 4 * ncol * nf, half), BF16),
            pltpu.VMEM((rpd, ncol, 2 * SG), F32),
            pltpu.VMEM((rpd, nc, COLS_DEV, 2 * SG), F32),
            pltpu.VMEM((rpd, nf, 2 * SG), F32),
            pltpu.SMEM((1,), I32), pltpu.SMEM((2,), I32), pltpu.SMEM((ncol,), I32),
            pltpu.SMEM((nf,), I32), pltpu.SMEM((nf,), I32),
            dma(()), dma((rpd,)), dma((2,)), dma(()), dma((rpd,)), dma((3,)), dma((5,)),
            pltpu.SemaphoreType.REGULAR,
        ],
        compiler_params=pltpu.CompilerParams(
            collective_id=0, has_side_effects=True, vmem_limit_bytes=24 << 20
        ),
        name="gather_columns",
    )(facet_x, *(
        pltpu.with_memory_space_constraint(z, pltpu.HBM)
        for z in (facet_y, col_u, slot_col[0], slot_v[0], facets.reshape(rows, 2, width))
    ))
    out = pl.pallas_call(
        v_kernel,
        out_shape=jax.ShapeDtypeStruct((SG, 2 * SG), F32),
        in_specs=[vm, vm, vm],
        out_specs=pl.BlockSpec(memory_space=pltpu.HBM),
        scratch_shapes=[
            pltpu.VMEM((lanes_of(tail), 2 * SG), BF16),
            pltpu.VMEM((SG, 2 * SG), F32),
            dma((SG // LANES,)),
        ],
        compiler_params=pltpu.CompilerParams(vmem_limit_bytes=24 << 20),
        name="v_transform",
    )(acc, h, e)
    return out[None, None]


def solution(mesh):
    placed = (
        P(None, "facet", None, None, "col"),
        P("facet"),
        P(),
        P(),
        P("col", None),
        P("col", None),
    )
    return jax.shard_map(
        functools.partial(per_device, mesh.shape["facet"], mesh.shape["col"]),
        mesh=mesh,
        in_specs=placed,
        out_specs=P("col", "facet", None, None),
        check_vma=False,
    )
```

time: 27.2 us -> 22.7 us (0.83)
  Pallas kernels: 26.4 us -> 21.9 us
    pallas_call x2, Pallas kernels: 26.4 us -> 21.9 us  [the longest x1 20.2 us: per_device(): pl.pallas_call(functools.partial(gather_kernel, nf, nc, img, band), out_s...]
where the time goes in v1:
time: 22.7 us; the launch traced here: 22.5 us
  Pallas kernels  21.9 us (96%)
  between operations  0.66 us (3%)
    pallas_call x1, Pallas kernels, per_device(): pl.pallas_call(functools.partial(gather_kernel, nf, nc, img, band), out_s...  20.2 us
    pallas_call x1, Pallas kernels, per_device(): pl.pallas_call(v_kernel, out_shape=jax.ShapeDtypeStruct((SG, 2 * SG), F32...  1.65 us

profile of v1, /device:TPU:0, one launch (start us, length us, event | category | flops | bytes accessed | tf_op | source)
XLA Modules:
  0.0 22.5 jit_solution(15910011775492877346)
XLA Ops:
  0.7 20.2 %gather_columns.1 = (f32[512,1024]{1,0:T(8,128)S(1)}, f32[16,1024]{1,0:T(8,128)S(1)}, bf16[512,128]{1,0:T(8,128)(2,1)S(1)}) custom-call(s32[1]{0:T(128)S(6)} %copy.7.fx_hbm, s32[2]{0:T(128)} %fy_hbm.1, s32[8]{0:T(128)} %u_hbm.1, s32[8]{0:T(128)} %bitcast.5, s32[8]{0:T(128)} %bitcast.6, f32[48,2,1024]{2,1,0:T(2,128)} %bitcast.4), custom_call_target="tpu_custom_call" | custom-call | tf_op jit(solution)/shard_map/gather_columns/pallas_call | solution.py:342
  20.9 1.7 %v_transform.1 = f32[512,1024]{1,0:T(8,128)} custom-call(f32[512,1024]{1,0:T(8,128)S(1)} %get-tuple-element.8.acc_ref, f32[16,1024]{1,0:T(8,128)S(1)} %get-tuple-element.9.h_ref, bf16[512,128]{1,0:T(8,128)(2,1)S(1)} %get-tuple-element.10.e_ref), custom_call_target="tpu_custom_call" | custom-call | tf_op jit(solution)/shard_map/v_transform/pallas_call | solution.py:379

commit v2 on v1

--- a/solution.py
+++ b/solution.py
@@ -57,6 +57,10 @@
     return index
 
 
+def far_first(count):
+    return sorted(range(1, count), key=lambda d: (-bin(d >> 1).count("1"), d & 1, d))
+
+
 def mirrored(pieces):
     rows = pieces[0].shape[0]
     lane = LANES - 1 - lax.broadcasted_iota(I32, (rows, LANES), 1)
@@ -83,11 +87,11 @@
 
 
 def gather_kernel(
-    nf, nc, img, band,
-    fx_hbm, fy_hbm, u_hbm, sc_hbm, sv_hbm, facets_ref,
+    nf, nc, img, band, away,
+    fx_ref, fy_hbm, u_hbm, sc_hbm, sv_hbm, facets_ref,
     acc_ref, h_ref, e_ref,
-    hbuf, e1, rhs, cells, fxs, fxall, table, premod, phase, eo, zbuf, part, zrecv, gsend,
-    fx_ref, fy_ref, u_ref, sc_ref, sv_ref,
+    vfac, f_sem, hbuf, e1, rhs, cells, fxs, fxall, table, premod, phase, eo, zbuf, part, zrecv, gsend,
+    fy_ref, u_ref, sc_ref, sv_ref,
     s_a2a, r_a2a, x_sem, s_z, r_z, g_sem, i_sem, z_sem,
 ):
     f = lax.axis_index("facet")
@@ -100,51 +104,76 @@
     depth = rpd * nf
     tail = h_ref.shape[0]
 
+    barrier = pltpu.get_barrier_semaphore()
+    for d in far_first(nf):
+        pl.semaphore_signal(barrier, inc=1, device_id=(partner(f, nf, d), c), device_id_type=MESH)
+
+    def tell_above(z, carry):
+        pl.semaphore_signal(barrier, inc=1, device_id=(f, z), device_id_type=MESH)
+        return carry
+
+    @pl.when(c < nc - 1)
+    def _():
+        for d in far_first(nf):
+            pl.semaphore_signal(barrier, inc=1, device_id=(partner(f, nf, d), c + 1), device_id_type=MESH)
+
+    lax.fori_loop(c + 1, nc, tell_above, 0)
+    for y in range(rpd):
+        for p in range(nf):
+            pltpu.make_async_copy(facets_ref.at[p * rpd + y], vfac.at[y, p], f_sem.at[y]).start()
     numbers = []
     for i, (src, dst) in enumerate((
-        (fx_hbm, fx_ref), (fy_hbm, fy_ref), (u_hbm, u_ref), (sc_hbm, sc_ref), (sv_hbm, sv_ref)
+        (fy_hbm, fy_ref), (u_hbm, u_ref), (sc_hbm, sc_ref), (sv_hbm, sv_ref)
     )):
         copy = pltpu.make_async_copy(src, dst, i_sem.at[i])
         copy.start()
         numbers.append(copy)
-    barrier = pltpu.get_barrier_semaphore()
-    for d in range(1, nf):
-        pl.semaphore_signal(barrier, inc=1, device_id=(partner(f, nf, d), c), device_id_type=MESH)
-
-    def tell_above(z, carry):
-        pl.semaphore_signal(barrier, inc=1, device_id=(f, z), device_id_type=MESH)
-        return carry
-
-    lax.fori_loop(c + 1, nc, tell_above, 0)
-    pl.semaphore_wait(barrier, nf - 1 + c)
+    fxs[...] = jnp.full(fxs.shape, fx_ref[0], I32)
+    pl.semaphore_wait(barrier, nf - 1 + c + jnp.where(c > 0, nf - 1, 0))
 
     def done(ref, sem):
         pltpu.make_async_copy(ref, ref, sem).wait()
 
-    numbers[0].wait()
-    fxs[...] = jnp.full(fxs.shape, fx_ref[0], I32)
-    for d in range(1, nf):
+    for d in far_first(nf):
         pltpu.make_async_remote_copy(
             src_ref=fxs, dst_ref=fxall.at[f], send_sem=x_sem.at[0], recv_sem=x_sem.at[1],
             device_id=(partner(f, nf, d), c), device_id_type=MESH,
         ).start()
     pltpu.make_async_copy(fxs, fxall.at[f], x_sem.at[1]).start()
-    for y in range(rpd):
-        for d in range(1, nf):
-            peer = partner(f, nf, d)
+
+    def distribute(y):
+        moved = y >= rpd - away
+        plane = jnp.where(c > 0, c - 1, 0) if moved else c
+        slot = jnp.where(c > 0, y + away, y) if moved else y
+        done(vfac.at[y], f_sem.at[y])
+
+        def send(peer):
             pltpu.make_async_remote_copy(
-                src_ref=facets_ref.at[peer * rpd + y], dst_ref=cells.at[y, :, f],
-                send_sem=s_a2a, recv_sem=r_a2a.at[y],
-                device_id=(peer, c), device_id_type=MESH,
+                src_ref=vfac.at[y, peer], dst_ref=cells.at[slot, :, f],
+                send_sem=s_a2a, recv_sem=r_a2a.at[slot],
+                device_id=(peer, plane), device_id_type=MESH,
             ).start()
-        pltpu.make_async_copy(facets_ref.at[f * rpd + y], cells.at[y, :, f], r_a2a.at[y]).start()
+
+        def keep():
+            pltpu.make_async_copy(vfac.at[y, f], cells.at[slot, :, f], r_a2a.at[slot]).start()
+
+        for d in far_first(nf):
+            send(partner(f, nf, d))
+        if moved:
+            pl.when(c > 0)(lambda: send(f))
+            pl.when(c == 0)(keep)
+        else:
+            keep()
+
+    for y in range(rpd - away):
+        distribute(y)
 
     def tell_below(z, carry):
         pl.semaphore_signal(z_sem, inc=1, device_id=(f, z), device_id_type=MESH)
         return carry
 
     lax.fori_loop(0, c, tell_below, 0)
-    for copy in numbers[1:]:
+    for copy in numbers:
         copy.wait()
 
     uv = jnp.zeros((ncol, half), I32)
@@ -168,6 +197,9 @@
         return carry
 
     lax.fori_loop(0, half // block, table_step, 0)
+
+    for y in range(rpd - away, rpd):
+        distribute(y)
 
     scale = 1.0 / math.sqrt(1.0 * rows * width * nc * nf)
     for target, first_row, count in ((e1, 0, depth - tail), (e_ref, depth - tail, tail)):
@@ -192,6 +224,7 @@
 
         lax.fori_loop(0, SG // block, v_step, 0)
 
+    part[...] = jnp.zeros_like(part)
     done(fxall, x_sem.at[1])
     lane = lax.broadcasted_iota(I32, (ncol, SG), 1)
     uv = jnp.zeros((ncol, SG), I32)
@@ -199,23 +232,30 @@
     for i in range(ncol):
         uv = jnp.where(row == i, u_ref[i], uv)
     ua = uv + jnp.where(lane < HALF, HALF + lane, SG - 1 - lane)
-    shift = 2 * c * width + width - 1
-
-    def phase_step(k, carry):
+
+    def phase_step(i, carry):
+        upper = jnp.where(i < nf, 0, 1)
+        k = i - upper * nf
         fx = jnp.broadcast_to(fxall[k], (ncol, LANES))
-        fx = jnp.concatenate([2 * fx + shift] * (SG // LANES), axis=1)
-        wc, ws = turn(ua * fx, 2 * img)
-        phase[0, k] = wc
-        phase[1, k] = ws
-        return carry
-
-    lax.fori_loop(0, nf, phase_step, 0)
+        fx = 2 * fx + ((2 * (c + upper) + 1) * width - 1)
+        wc, ws = turn(ua * jnp.concatenate([fx] * (SG // LANES), axis=1), 2 * img)
+        phase[upper, 0, k] = wc
+        phase[upper, 1, k] = ws
+        return carry
+
+    lax.fori_loop(0, jnp.where(c < nc - 1, 2 * nf, nf), phase_step, 0)
+
     nt = half // LANES
 
-    def row_step(y, carry):
-        done(cells.at[y], r_a2a.at[y])
+    own = jnp.where(c > 0, rpd - away, rpd)
+
+    def row_step(i, carry):
+        late = jnp.where(i < own, 0, 1)
+        slot = i + late * (rpd - own)
+        y = i - late * (own - (rpd - away))
+        done(cells.at[slot], r_a2a.at[slot])
         for m in range(2):
-            value = cells[y, m]
+            value = cells[slot, m]
             upper = tiles(value, half, nt)
             lower = mirrored(tiles(value, 0, nt))
             for j in range(nt):
@@ -239,50 +279,53 @@
         for n in range(2):
             both = mm(zbuf[n], table[n, 0])
             prod.append(both[:size] + both[size:] + mm(zbuf[n, :size, :], table[n, 1]))
-        re = jnp.zeros((ncol, SG), F32)
-        im = jnp.zeros((ncol, SG), F32)
+        re = part[y, :, 0:SG]
+        im = part[y, :, SG:2 * SG]
         for k in range(nf):
             at = 2 * k * ncol
             rc, ic = prod[0][at:at + ncol], prod[0][at + ncol:at + 2 * ncol]
             rs, is_ = prod[1][at:at + ncol], prod[1][at + ncol:at + 2 * ncol]
             hr = jnp.concatenate([rc + is_, rc - is_], axis=1)
             hm = jnp.concatenate([ic - rs, ic + rs], axis=1)
-            wc = phase[0, k]
-            ws = phase[1, k]
+            wc = phase[late, 0, k]
+            ws = phase[late, 1, k]
             re = re + (hr * wc + hm * ws)
             im = im + (hm * wc - hr * ws)
         part[y, :, 0:SG] = re
         part[y, :, SG:2 * SG] = im
 
-        @pl.when((y == 0) & (c < nc - 1))
+        @pl.when((i == 0) & (c < nc - 1))
         def _():
             pl.semaphore_wait(z_sem, nc - 1 - c)
 
-        for d in range(nc - 1):
-            owner = jnp.where(d < c, d, d + 1)
-            pltpu.make_async_remote_copy(
-                src_ref=part.at[y, pl.ds(owner * COLS_DEV, COLS_DEV)], dst_ref=zrecv.at[y, c],
-                send_sem=s_z, recv_sem=r_z.at[y],
-                device_id=(f, owner), device_id_type=MESH,
+        @pl.when((c > 0) | (i < rpd - away) | (i >= rpd))
+        def share():
+            for d in range(nc - 1):
+                owner = jnp.where(d < c, d, d + 1)
+                pltpu.make_async_remote_copy(
+                    src_ref=part.at[y, pl.ds(owner * COLS_DEV, COLS_DEV)], dst_ref=zrecv.at[y, c],
+                    send_sem=s_z, recv_sem=r_z.at[y],
+                    device_id=(f, owner), device_id_type=MESH,
+                ).start()
+            pltpu.make_async_copy(
+                part.at[y, pl.ds(c * COLS_DEV, COLS_DEV)], zrecv.at[y, c], r_z.at[y]
             ).start()
-        pltpu.make_async_copy(
-            part.at[y, pl.ds(c * COLS_DEV, COLS_DEV)], zrecv.at[y, c], r_z.at[y]
-        ).start()
-        return carry
-
-    lax.fori_loop(0, rpd, row_step, 0)
+
+        return carry
+
+    lax.fori_loop(0, own + jnp.where(c < nc - 1, away, 0), row_step, 0)
 
     slot = lax.broadcasted_iota(I32, (nf, SG), 0)
     which = jnp.zeros((nf, SG), I32)
-    for d in range(nf):
-        which = jnp.where(slot == d, sc_ref[partner(f, nf, d)], which)
+    for p in range(nf):
+        which = jnp.where(slot == p, sc_ref[p], which)
 
     nh = HALF // LANES
 
-    def sum_step(target, y0, sem, y, carry):
-        done(zrecv.at[y], r_z.at[y])
+    def sum_step(target, y0, sem, planes, y, carry):
+        done(zrecv.at[y, pl.ds(0, planes)], r_z.at[y])
         acc = zrecv[y, 0]
-        for d in range(1, nc):
+        for d in range(1, planes):
             acc = acc + zrecv[y, d]
         for m in range(2):
             value = acc[:, m * SG:(m + 1) * SG]
@@ -292,37 +335,52 @@
             upper = tiles(chosen, 0, nh)
             lower = mirrored(tiles(chosen, HALF, nh))
             gsend[y, :, m * SG:(m + 1) * SG] = jnp.concatenate(lower + upper, axis=1)
-        for d in range(1, nf):
+        for i in range(nf - 1):
+            peer = jnp.where(i < f, i, i + 1)
             pltpu.make_async_remote_copy(
-                src_ref=gsend.at[y, d], dst_ref=target.at[(y - y0) * nf + f],
+                src_ref=gsend.at[y, peer], dst_ref=target.at[(y - y0) * nf + f],
                 send_sem=g_sem.at[0], recv_sem=sem,
-                device_id=(partner(f, nf, d), c), device_id_type=MESH,
+                device_id=(peer, c), device_id_type=MESH,
             ).start()
-        pltpu.make_async_copy(gsend.at[y, 0], target.at[(y - y0) * nf + f], sem).start()
+        pltpu.make_async_copy(gsend.at[y, f], target.at[(y - y0) * nf + f], sem).start()
         return carry
 
     cut = rpd - tail // nf
-    lax.fori_loop(0, cut, functools.partial(sum_step, hbuf, 0, g_sem.at[1]), 0)
-    lax.fori_loop(cut, rpd, functools.partial(sum_step, h_ref, cut, g_sem.at[2]), 0)
+    lax.fori_loop(0, cut, functools.partial(sum_step, hbuf, 0, g_sem.at[1], nc), 0)
+    lax.fori_loop(cut, rpd - away, functools.partial(sum_step, h_ref, cut, g_sem.at[2], nc), 0)
+    lax.fori_loop(rpd - away, rpd, functools.partial(sum_step, h_ref, cut, g_sem.at[2], nc - 1), 0)
     done(hbuf, g_sem.at[1])
     stack(hbuf, rhs)
     acc_ref[...] = mm(e1[...], rhs[...])
     done(h_ref, g_sem.at[2])
     done(fxall.at[pl.ds(0, nf - 1)], x_sem.at[0])
     done(facets_ref.at[pl.ds(0, (nf - 1) * rpd)], s_a2a)
-    done(zrecv.at[:, pl.ds(1, nc - 1)], s_z)
+
+    @pl.when(c > 0)
+    def _():
+        done(facets_ref.at[pl.ds(0, away)], s_a2a)
+
+    done(zrecv.at[pl.ds(0, rpd - away), pl.ds(1, nc - 1)], s_z)
+
+    @pl.when(c < nc - 1)
+    def _():
+        done(zrecv.at[pl.ds(0, away), pl.ds(1, nc - 1)], s_z)
+
     done(facets_ref.at[pl.ds(0, (nf - 1) * rpd * SG // width)], g_sem.at[0])
 
 
 def v_kernel(acc_ref, h_ref, e_ref, out_ref, rhs, buf, sem):
     stack(h_ref, rhs)
     copies = []
-    chunk = 2 * LANES
-    for i in range(2 * SG // chunk):
-        at = pl.ds(i * chunk, chunk)
-        buf[:, at] = acc_ref[:, at] + mm(e_ref[...], rhs[:, at])
-        copies.append(pltpu.make_async_copy(buf.at[:, at], out_ref.at[:, at], sem.at[i]))
+    n = 0
+    first = 0
+    for chunk in (128,)*4:
+        at = pl.ds(first, chunk)
+        buf[at, :] = acc_ref[at, :] + mm(e_ref[at, :], rhs[...])
+        copies.append(pltpu.make_async_copy(buf.at[at], out_ref.at[at], sem.at[n]))
         copies[-1].start()
+        n += 1
+        first += chunk
     for copy in copies:
         copy.wait()
 
@@ -337,35 +395,37 @@
     depth = rpd * nf
     half = width // 2
     tail = (rpd - 2 * rpd // 3) * nf
+    away = 1
     vm = pl.BlockSpec(memory_space=pltpu.VMEM)
     dma = pltpu.SemaphoreType.DMA
     acc, h, e = pl.pallas_call(
-        functools.partial(gather_kernel, nf, nc, img, band),
+        functools.partial(gather_kernel, nf, nc, img, band, away),
         out_shape=(
             jax.ShapeDtypeStruct((SG, 2 * SG), F32),
             jax.ShapeDtypeStruct((tail, 2 * SG), F32),
             jax.ShapeDtypeStruct((SG, lanes_of(tail)), BF16),
         ),
-        in_specs=[pl.BlockSpec(memory_space=pl.ANY)] + [pl.BlockSpec(memory_space=pltpu.HBM)] * 5,
+        in_specs=[pl.BlockSpec(memory_space=pltpu.SMEM)] + [pl.BlockSpec(memory_space=pltpu.HBM)] * 5,
         out_specs=(vm, vm, vm),
         scratch_shapes=[
+            pltpu.VMEM((rpd, nf, 2, width), F32), dma((rpd,)),
             pltpu.VMEM((depth - tail, 2 * SG), F32),
             pltpu.VMEM((SG, lanes_of(depth - tail)), BF16),
             pltpu.VMEM((lanes_of(depth - tail), 2 * SG), BF16),
-            pltpu.VMEM((rpd, 2, nf, width), F32),
+            pltpu.VMEM((rpd + away, 2, nf, width), F32),
             pltpu.VMEM((1, LANES), I32),
             pltpu.VMEM((nf, 1, LANES), I32),
             pltpu.VMEM((2, 2, half, HALF), BF16),
             pltpu.VMEM((2, ncol, half), F32),
-            pltpu.VMEM((2, nf, ncol, SG), F32),
+            pltpu.VMEM((2, 2, nf, ncol, SG), F32),
             pltpu.VMEM((4, nf, half), F32),
             pltpu.VMEM((2, 4 * ncol * nf, half), BF16),
             pltpu.VMEM((rpd, ncol, 2 * SG), F32),
             pltpu.VMEM((rpd, nc, COLS_DEV, 2 * SG), F32),
             pltpu.VMEM((rpd, nf, 2 * SG), F32),
-            pltpu.SMEM((1,), I32), pltpu.SMEM((2,), I32), pltpu.SMEM((ncol,), I32),
+            pltpu.SMEM((2,), I32), pltpu.SMEM((ncol,), I32),
             pltpu.SMEM((nf,), I32), pltpu.SMEM((nf,), I32),
-            dma(()), dma((rpd,)), dma((2,)), dma(()), dma((rpd,)), dma((3,)), dma((5,)),
+            dma(()), dma((rpd + away,)), dma((2,)), dma(()), dma((rpd,)), dma((3,)), dma((4,)),
             pltpu.SemaphoreType.REGULAR,
         ],
         compiler_params=pltpu.CompilerParams(
@@ -384,7 +444,7 @@
         scratch_shapes=[
             pltpu.VMEM((lanes_of(tail), 2 * SG), BF16),
             pltpu.VMEM((SG, 2 * SG), F32),
-            dma((SG // LANES,)),
+            dma((4,)),
         ],
         compiler_params=pltpu.CompilerParams(vmem_limit_bytes=24 << 20),
         name="v_transform",

time: 22.7 us -> 21.8 us (0.960)
  Pallas kernels: 21.9 us -> 21 us
    pallas_call x1, Pallas kernels: 20.2 us -> 19.4 us  [per_device(): pl.pallas_call(functools.partial(gather_kernel, nf, nc, img, band, away),...]
where the time goes in v2:
time: 21.8 us; the launch traced here: 21.7 us
  Pallas kernels  21 us (96%)
  between operations  0.66 us (3%)
    pallas_call x1, Pallas kernels, per_device(): pl.pallas_call(functools.partial(gather_kernel, nf, nc, img, band, away),...  19.4 us
    pallas_call x1, Pallas kernels, per_device(): pl.pallas_call(v_kernel, out_shape=jax.ShapeDtypeStruct((SG, 2 * SG), F32...  1.57 us

profile of v2, /device:TPU:0, one launch (start us, length us, event | category | flops | bytes accessed | tf_op | source)
XLA Modules:
  0.0 21.7 jit_solution(17675206731043959071)
XLA Ops:
  0.7 19.4 %gather_columns.1 = (f32[512,1024]{1,0:T(8,128)S(1)}, f32[16,1024]{1,0:T(8,128)S(1)}, bf16[512,128]{1,0:T(8,128)(2,1)S(1)}) custom-call(s32[1]{0:T(128)S(6)} %copy.7.fx_ref, s32[2]{0:T(128)} %fy_hbm.1, s32[8]{0:T(128)} %u_hbm.1, s32[8]{0:T(128)} %bitcast.5, s32[8]{0:T(128)} %bitcast.6, f32[48,2,1024]{2,1,0:T(2,128)} %bitcast.4), custom_call_target="tpu_custom_call" | custom-call | tf_op jit(solution)/shard_map/gather_columns/pallas_call | solution.py:401
  20.1 1.6 %v_transform.1 = f32[512,1024]{1,0:T(8,128)} custom-call(f32[512,1024]{1,0:T(8,128)S(1)} %get-tuple-element.8.acc_ref, f32[16,1024]{1,0:T(8,128)S(1)} %get-tuple-element.9.h_ref, bf16[512,128]{1,0:T(8,128)(2,1)S(1)} %get-tuple-element.10.e_ref), custom_call_target="tpu_custom_call" | custom-call | tf_op jit(solution)/shard_map/v_transform/pallas_call | solution.py:439

commit v3 on v2

--- a/solution.py
+++ b/solution.py
@@ -87,7 +87,7 @@
 
 
 def gather_kernel(
-    nf, nc, img, band, away,
+    nf, nc, img, band, lean,
     fx_ref, fy_hbm, u_hbm, sc_hbm, sv_hbm, facets_ref,
     acc_ref, h_ref, e_ref,
     vfac, f_sem, hbuf, e1, rhs, cells, fxs, fxall, table, premod, phase, eo, zbuf, part, zrecv, gsend,
@@ -103,6 +103,24 @@
     ncol = COLS_DEV * nc
     depth = rpd * nf
     tail = h_ref.shape[0]
+    cut = rpd - tail // nf
+    most = rpd + lean
+    part_of = nf // 4
+
+    def first_row(p):
+        return p * rpd + lean * (jnp.minimum(p, part_of) - jnp.maximum(p - (nf - part_of), 0))
+
+    def count_of(p):
+        return rpd + lean * (jnp.where(p < part_of, 1, 0) - jnp.where(p >= nf - part_of, 1, 0))
+
+    def both_of(p):
+        return (
+            p * rpd + lean * (min(p, part_of) - max(p - (nf - part_of), 0)),
+            rpd + lean * ((p < part_of) - (p >= nf - part_of)),
+        )
+
+    start = first_row(f)
+    count = count_of(f)
 
     barrier = pltpu.get_barrier_semaphore()
     for d in far_first(nf):
@@ -118,9 +136,13 @@
             pl.semaphore_signal(barrier, inc=1, device_id=(partner(f, nf, d), c + 1), device_id_type=MESH)
 
     lax.fori_loop(c + 1, nc, tell_above, 0)
-    for y in range(rpd):
+    for y in range(most):
         for p in range(nf):
-            pltpu.make_async_copy(facets_ref.at[p * rpd + y], vfac.at[y, p], f_sem.at[y]).start()
+            row, n = both_of(p)
+            if y < n:
+                pltpu.make_async_copy(
+                    facets_ref.at[row + y], vfac.at[row + y], f_sem.at[min(y, 1)]
+                ).start()
     numbers = []
     for i, (src, dst) in enumerate((
         (fy_hbm, fy_ref), (u_hbm, u_ref), (sc_hbm, sc_ref), (sv_hbm, sv_ref)
@@ -141,32 +163,32 @@
         ).start()
     pltpu.make_async_copy(fxs, fxall.at[f], x_sem.at[1]).start()
 
-    def distribute(y):
-        moved = y >= rpd - away
-        plane = jnp.where(c > 0, c - 1, 0) if moved else c
-        slot = jnp.where(c > 0, y + away, y) if moved else y
-        done(vfac.at[y], f_sem.at[y])
-
-        def send(peer):
-            pltpu.make_async_remote_copy(
-                src_ref=vfac.at[y, peer], dst_ref=cells.at[slot, :, f],
-                send_sem=s_a2a, recv_sem=r_a2a.at[slot],
-                device_id=(peer, plane), device_id_type=MESH,
-            ).start()
-
-        def keep():
-            pltpu.make_async_copy(vfac.at[y, f], cells.at[slot, :, f], r_a2a.at[slot]).start()
-
+    def send(row, peer, plane, slot):
+        pltpu.make_async_remote_copy(
+            src_ref=vfac.at[row], dst_ref=cells.at[slot, :, f],
+            send_sem=s_a2a, recv_sem=r_a2a.at[slot],
+            device_id=(peer, plane), device_id_type=MESH,
+        ).start()
+
+    def keep(row, slot):
+        pltpu.make_async_copy(vfac.at[row], cells.at[slot, :, f], r_a2a.at[slot]).start()
+
+    for y in range(most - 1):
+        if y < 2:
+            done(vfac.at[pl.ds(0, nf if y == 0 else rows - nf)], f_sem.at[y])
+        sure = y < rpd - lean - 1
         for d in far_first(nf):
-            send(partner(f, nf, d))
-        if moved:
-            pl.when(c > 0)(lambda: send(f))
-            pl.when(c == 0)(keep)
+            peer = partner(f, nf, d)
+            if sure:
+                send(first_row(peer) + y, peer, c, y)
+            else:
+                pl.when(y < count_of(peer) - 1)(
+                    functools.partial(send, first_row(peer) + y, peer, c, y)
+                )
+        if sure:
+            keep(start + y, y)
         else:
-            keep()
-
-    for y in range(rpd - away):
-        distribute(y)
+            pl.when(y < count - 1)(functools.partial(keep, start + y, y))
 
     def tell_below(z, carry):
         pl.semaphore_signal(z_sem, inc=1, device_id=(f, z), device_id_type=MESH)
@@ -198,18 +220,33 @@
 
     lax.fori_loop(0, half // block, table_step, 0)
 
-    for y in range(rpd - away, rpd):
-        distribute(y)
+    plane = jnp.where(c > 0, c - 1, 0)
+    for d in far_first(nf):
+        peer = partner(f, nf, d)
+        last = count_of(peer) - 1
+        send(first_row(peer) + last, peer, plane, jnp.where(c > 0, most, last))
+    pl.when(c > 0)(functools.partial(send, start + count - 1, f, plane, most))
+    pl.when(c == 0)(functools.partial(keep, start + count - 1, count - 1))
 
     scale = 1.0 / math.sqrt(1.0 * rows * width * nc * nf)
-    for target, first_row, count in ((e1, 0, depth - tail), (e_ref, depth - tail, tail)):
+    places = [], []
+    for y in range(most):
+        for p in range(nf):
+            row, n = both_of(p)
+            if y < n:
+                late = y >= cut
+                places[late].append((row - cut * p + y - cut if late else y * nf + p, row + y))
+    for target, spots in zip((e1, e_ref), places):
+        size = len(spots)
         lanes = target.shape[1]
         q = lax.broadcasted_iota(I32, (1, lanes), 1)
-        term = lax.div(q, 2 * count)
-        inner = q - term * (2 * count)
-        quarter = jnp.where(inner < count, 0, img // 4)
-        at = jnp.where(inner < count, inner, inner - count) + first_row
-        g = lax.rem(at, nf) * rpd + lax.div(at, nf)
+        term = lax.div(q, 2 * size)
+        inner = q - term * (2 * size)
+        quarter = jnp.where(inner < size, 0, img // 4)
+        at = jnp.where(inner < size, inner, inner - size)
+        g = jnp.zeros((1, lanes), I32)
+        for spot, row in spots:
+            g = jnp.where(at == spot, row, g)
         cell = jnp.where(g < band, fy_ref[0] + g, fy_ref[1] + g - band)
         cell, quarter, term = (jnp.broadcast_to(z, (block, lanes)) for z in (cell, quarter, term))
 
@@ -247,12 +284,12 @@
 
     nt = half // LANES
 
-    own = jnp.where(c > 0, rpd - away, rpd)
+    own = count - jnp.where(c > 0, 1, 0)
 
     def row_step(i, carry):
         late = jnp.where(i < own, 0, 1)
-        slot = i + late * (rpd - own)
-        y = i - late * (own - (rpd - away))
+        slot = jnp.where(i < own, i, most)
+        y = jnp.where(i < own, i, count - 1)
         done(cells.at[slot], r_a2a.at[slot])
         for m in range(2):
             value = cells[slot, m]
@@ -298,7 +335,7 @@
         def _():
             pl.semaphore_wait(z_sem, nc - 1 - c)
 
-        @pl.when((c > 0) | (i < rpd - away) | (i >= rpd))
+        @pl.when((c > 0) | (i < count - 1) | (i >= count))
         def share():
             for d in range(nc - 1):
                 owner = jnp.where(d < c, d, d + 1)
@@ -313,7 +350,7 @@
 
         return carry
 
-    lax.fori_loop(0, own + jnp.where(c < nc - 1, away, 0), row_step, 0)
+    lax.fori_loop(0, own + jnp.where(c < nc - 1, 1, 0), row_step, 0)
 
     slot = lax.broadcasted_iota(I32, (nf, SG), 0)
     which = jnp.zeros((nf, SG), I32)
@@ -322,7 +359,12 @@
 
     nh = HALF // LANES
 
-    def sum_step(target, y0, sem, planes, y, carry):
+    tail_row = start - cut * f
+
+    def sum_step(early, planes, y, carry):
+        target = hbuf if early else h_ref
+        place = y * nf + f if early else tail_row + y - cut
+        sem = g_sem.at[1 if early else 2]
         done(zrecv.at[y, pl.ds(0, planes)], r_z.at[y])
         acc = zrecv[y, 0]
         for d in range(1, planes):
@@ -338,35 +380,40 @@
         for i in range(nf - 1):
             peer = jnp.where(i < f, i, i + 1)
             pltpu.make_async_remote_copy(
-                src_ref=gsend.at[y, peer], dst_ref=target.at[(y - y0) * nf + f],
+                src_ref=gsend.at[y, peer], dst_ref=target.at[place],
                 send_sem=g_sem.at[0], recv_sem=sem,
                 device_id=(peer, c), device_id_type=MESH,
             ).start()
-        pltpu.make_async_copy(gsend.at[y, f], target.at[(y - y0) * nf + f], sem).start()
+        pltpu.make_async_copy(gsend.at[y, f], target.at[place], sem).start()
         return carry
 
-    cut = rpd - tail // nf
-    lax.fori_loop(0, cut, functools.partial(sum_step, hbuf, 0, g_sem.at[1], nc), 0)
-    lax.fori_loop(cut, rpd - away, functools.partial(sum_step, h_ref, cut, g_sem.at[2], nc), 0)
-    lax.fori_loop(rpd - away, rpd, functools.partial(sum_step, h_ref, cut, g_sem.at[2], nc - 1), 0)
+    lax.fori_loop(0, jnp.minimum(cut, count - 1), functools.partial(sum_step, True, nc), 0)
+    lax.fori_loop(cut, count - 1, functools.partial(sum_step, False, nc), 0)
+    if rpd - lean <= cut:
+        @pl.when(count <= cut)
+        def _():
+            sum_step(True, nc - 1, count - 1, 0)
+
+    @pl.when(count > cut)
+    def _():
+        sum_step(False, nc - 1, count - 1, 0)
+
+    def drain(ref, sem, times):
+        def step(i, carry):
+            done(ref, sem)
+            return carry
+
+        lax.fori_loop(0, times, step, 0)
+
+    done(fxall.at[pl.ds(0, nf - 1)], x_sem.at[0])
+    done(facets_ref.at[pl.ds(0, rows - most)], s_a2a)
+    drain(facets_ref.at[pl.ds(0, 1)], s_a2a, most - own)
+    drain(zrecv.at[0, pl.ds(1, nc - 1)], s_z, count - jnp.where(c < nc - 1, 0, 1))
     done(hbuf, g_sem.at[1])
     stack(hbuf, rhs)
     acc_ref[...] = mm(e1[...], rhs[...])
+    drain(facets_ref.at[pl.ds(0, (nf - 1) * 2 * SG // width), 0], g_sem.at[0], count)
     done(h_ref, g_sem.at[2])
-    done(fxall.at[pl.ds(0, nf - 1)], x_sem.at[0])
-    done(facets_ref.at[pl.ds(0, (nf - 1) * rpd)], s_a2a)
-
-    @pl.when(c > 0)
-    def _():
-        done(facets_ref.at[pl.ds(0, away)], s_a2a)
-
-    done(zrecv.at[pl.ds(0, rpd - away), pl.ds(1, nc - 1)], s_z)
-
-    @pl.when(c < nc - 1)
-    def _():
-        done(zrecv.at[pl.ds(0, away), pl.ds(1, nc - 1)], s_z)
-
-    done(facets_ref.at[pl.ds(0, (nf - 1) * rpd * SG // width)], g_sem.at[0])
 
 
 def v_kernel(acc_ref, h_ref, e_ref, out_ref, rhs, buf, sem):
@@ -394,12 +441,12 @@
     ncol = COLS_DEV * nc
     depth = rpd * nf
     half = width // 2
-    tail = (rpd - 2 * rpd // 3) * nf
-    away = 1
+    tail = (rpd - rpd // 2) * nf
+    lean = rpd // 6
     vm = pl.BlockSpec(memory_space=pltpu.VMEM)
     dma = pltpu.SemaphoreType.DMA
     acc, h, e = pl.pallas_call(
-        functools.partial(gather_kernel, nf, nc, img, band, away),
+        functools.partial(gather_kernel, nf, nc, img, band, lean),
         out_shape=(
             jax.ShapeDtypeStruct((SG, 2 * SG), F32),
             jax.ShapeDtypeStruct((tail, 2 * SG), F32),
@@ -408,11 +455,11 @@
         in_specs=[pl.BlockSpec(memory_space=pltpu.SMEM)] + [pl.BlockSpec(memory_space=pltpu.HBM)] * 5,
         out_specs=(vm, vm, vm),
         scratch_shapes=[
-            pltpu.VMEM((rpd, nf, 2, width), F32), dma((rpd,)),
+            pltpu.VMEM((rows, 2, width), F32), dma((2,)),
             pltpu.VMEM((depth - tail, 2 * SG), F32),
             pltpu.VMEM((SG, lanes_of(depth - tail)), BF16),
             pltpu.VMEM((lanes_of(depth - tail), 2 * SG), BF16),
-            pltpu.VMEM((rpd + away, 2, nf, width), F32),
+            pltpu.VMEM((rpd + lean + 1, 2, nf, width), F32),
             pltpu.VMEM((1, LANES), I32),
             pltpu.VMEM((nf, 1, LANES), I32),
             pltpu.VMEM((2, 2, half, HALF), BF16),
@@ -420,12 +467,12 @@
             pltpu.VMEM((2, 2, nf, ncol, SG), F32),
             pltpu.VMEM((4, nf, half), F32),
             pltpu.VMEM((2, 4 * ncol * nf, half), BF16),
-            pltpu.VMEM((rpd, ncol, 2 * SG), F32),
-            pltpu.VMEM((rpd, nc, COLS_DEV, 2 * SG), F32),
-            pltpu.VMEM((rpd, nf, 2 * SG), F32),
+            pltpu.VMEM((rpd + lean, ncol, 2 * SG), F32),
+            pltpu.VMEM((rpd + lean, nc, COLS_DEV, 2 * SG), F32),
+            pltpu.VMEM((rpd + lean, nf, 2 * SG), F32),
             pltpu.SMEM((2,), I32), pltpu.SMEM((ncol,), I32),
             pltpu.SMEM((nf,), I32), pltpu.SMEM((nf,), I32),
-            dma(()), dma((rpd + away,)), dma((2,)), dma(()), dma((rpd,)), dma((3,)), dma((4,)),
+            dma(()), dma((rpd + lean + 1,)), dma((2,)), dma(()), dma((rpd + lean,)), dma((3,)), dma((4,)),
             pltpu.SemaphoreType.REGULAR,
         ],
         compiler_params=pltpu.CompilerParams(

time: 21.8 us -> 21.1 us (0.968)
  Pallas kernels: 21 us -> 20.3 us
    pallas_call x1, Pallas kernels: 19.4 us -> 18.7 us  [per_device(): pl.pallas_call(functools.partial(gather_kernel, nf, nc, img, band, lean),...]
where the time goes in v3:
time: 21.1 us; the launch traced here: 21 us
  Pallas kernels  20.3 us (96%)
  between operations  0.66 us (3%)
    pallas_call x1, Pallas kernels, per_device(): pl.pallas_call(functools.partial(gather_kernel, nf, nc, img, band, lean),...  18.7 us
    pallas_call x1, Pallas kernels, per_device(): pl.pallas_call(v_kernel, out_shape=jax.ShapeDtypeStruct((SG, 2 * SG), F32...  1.59 us

profile of v3, /device:TPU:0, one launch (start us, length us, event | category | flops | bytes accessed | tf_op | source)
XLA Modules:
  0.0 21.0 jit_solution(5779109537477226762)
XLA Ops:
  0.7 18.7 %gather_columns.1 = (f32[512,1024]{1,0:T(8,128)S(1)}, f32[24,1024]{1,0:T(8,128)S(1)}, bf16[512,256]{1,0:T(8,128)(2,1)S(1)}) custom-call(s32[1]{0:T(128)S(6)} %copy.7.fx_ref, s32[2]{0:T(128)} %fy_hbm.1, s32[8]{0:T(128)} %u_hbm.1, s32[8]{0:T(128)} %bitcast.5, s32[8]{0:T(128)} %bitcast.6, f32[48,2,1024]{2,1,0:T(2,128)} %bitcast.4), custom_call_target="tpu_custom_call" | custom-call | tf_op jit(solution)/shard_map/gather_columns/pallas_call | solution.py:448
  19.4 1.6 %v_transform.1 = f32[512,1024]{1,0:T(8,128)} custom-call(f32[512,1024]{1,0:T(8,128)S(1)} %get-tuple-element.8.acc_ref, f32[24,1024]{1,0:T(8,128)S(1)} %get-tuple-element.9.h_ref, bf16[512,256]{1,0:T(8,128)(2,1)S(1)} %get-tuple-element.10.e_ref), custom_call_target="tpu_custom_call" | custom-call | tf_op jit(solution)/shard_map/v_transform/pallas_call | solution.py:486

commit v4 on v3

--- a/solution.py
+++ b/solution.py
@@ -87,7 +87,7 @@
 
 
 def gather_kernel(
-    nf, nc, img, band, lean,
+    nf, nc, img, band, lean, tilt,
     fx_ref, fy_hbm, u_hbm, sc_hbm, sv_hbm, facets_ref,
     acc_ref, h_ref, e_ref,
     vfac, f_sem, hbuf, e1, rhs, cells, fxs, fxall, table, premod, phase, eo, zbuf, part, zrecv, gsend,
@@ -104,19 +104,22 @@
     depth = rpd * nf
     tail = h_ref.shape[0]
     cut = rpd - tail // nf
-    most = rpd + lean
+    most = rpd + lean + tilt
+    least = rpd - lean - tilt
     part_of = nf // 4
 
     def first_row(p):
-        return p * rpd + lean * (jnp.minimum(p, part_of) - jnp.maximum(p - (nf - part_of), 0))
+        shift = jnp.minimum(p, part_of) - jnp.maximum(p - (nf - part_of), 0)
+        return p * rpd + lean * shift - tilt * lax.rem(p, 2)
 
     def count_of(p):
-        return rpd + lean * (jnp.where(p < part_of, 1, 0) - jnp.where(p >= nf - part_of, 1, 0))
+        more = jnp.where(p < part_of, 1, 0) - jnp.where(p >= nf - part_of, 1, 0)
+        return rpd + lean * more + tilt * (2 * lax.rem(p, 2) - 1)
 
     def both_of(p):
         return (
-            p * rpd + lean * (min(p, part_of) - max(p - (nf - part_of), 0)),
-            rpd + lean * ((p < part_of) - (p >= nf - part_of)),
+            p * rpd + lean * (min(p, part_of) - max(p - (nf - part_of), 0)) - tilt * (p % 2),
+            rpd + lean * ((p < part_of) - (p >= nf - part_of)) + tilt * (2 * (p % 2) - 1),
         )
 
     start = first_row(f)
@@ -176,7 +179,7 @@
     for y in range(most - 1):
         if y < 2:
             done(vfac.at[pl.ds(0, nf if y == 0 else rows - nf)], f_sem.at[y])
-        sure = y < rpd - lean - 1
+        sure = y < least - 1
         for d in far_first(nf):
             peer = partner(f, nf, d)
             if sure:
@@ -389,7 +392,7 @@
 
     lax.fori_loop(0, jnp.minimum(cut, count - 1), functools.partial(sum_step, True, nc), 0)
     lax.fori_loop(cut, count - 1, functools.partial(sum_step, False, nc), 0)
-    if rpd - lean <= cut:
+    if least <= cut:
         @pl.when(count <= cut)
         def _():
             sum_step(True, nc - 1, count - 1, 0)
@@ -441,12 +444,13 @@
     ncol = COLS_DEV * nc
     depth = rpd * nf
     half = width // 2
-    tail = (rpd - rpd // 2) * nf
+    tail = (rpd - rpd // 3) * nf
     lean = rpd // 6
+    tilt = 1
     vm = pl.BlockSpec(memory_space=pltpu.VMEM)
     dma = pltpu.SemaphoreType.DMA
     acc, h, e = pl.pallas_call(
-        functools.partial(gather_kernel, nf, nc, img, band, lean),
+        functools.partial(gather_kernel, nf, nc, img, band, lean, tilt),
         out_shape=(
             jax.ShapeDtypeStruct((SG, 2 * SG), F32),
             jax.ShapeDtypeStruct((tail, 2 * SG), F32),
@@ -459,7 +463,7 @@
             pltpu.VMEM((depth - tail, 2 * SG), F32),
             pltpu.VMEM((SG, lanes_of(depth - tail)), BF16),
             pltpu.VMEM((lanes_of(depth - tail), 2 * SG), BF16),
-            pltpu.VMEM((rpd + lean + 1, 2, nf, width), F32),
+            pltpu.VMEM((rpd + lean + tilt + 1, 2, nf, width), F32),
             pltpu.VMEM((1, LANES), I32),
             pltpu.VMEM((nf, 1, LANES), I32),
             pltpu.VMEM((2, 2, half, HALF), BF16),
@@ -467,12 +471,12 @@
             pltpu.VMEM((2, 2, nf, ncol, SG), F32),
             pltpu.VMEM((4, nf, half), F32),
             pltpu.VMEM((2, 4 * ncol * nf, half), BF16),
-            pltpu.VMEM((rpd + lean, ncol, 2 * SG), F32),
-            pltpu.VMEM((rpd + lean, nc, COLS_DEV, 2 * SG), F32),
-            pltpu.VMEM((rpd + lean, nf, 2 * SG), F32),
+            pltpu.VMEM((rpd + lean + tilt, ncol, 2 * SG), F32),
+            pltpu.VMEM((rpd + lean + tilt, nc, COLS_DEV, 2 * SG), F32),
+            pltpu.VMEM((rpd + lean + tilt, nf, 2 * SG), F32),
             pltpu.SMEM((2,), I32), pltpu.SMEM((ncol,), I32),
             pltpu.SMEM((nf,), I32), pltpu.SMEM((nf,), I32),
-            dma(()), dma((rpd + lean + 1,)), dma((2,)), dma(()), dma((rpd + lean,)), dma((3,)), dma((4,)),
+            dma(()), dma((rpd + lean + tilt + 1,)), dma((2,)), dma(()), dma((rpd + lean + tilt,)), dma((3,)), dma((4,)),
             pltpu.SemaphoreType.REGULAR,
         ],
         compiler_params=pltpu.CompilerParams(

time: 21.1 us -> 20.6 us (0.976)
  Pallas kernels: 20.3 us -> 19.8 us
    pallas_call x1, Pallas kernels: 18.7 us -> 18.2 us  [per_device(): pl.pallas_call(functools.partial(gather_kernel, nf, nc, img, band, lean,...]
where the time goes in v4:
time: 20.6 us; the launch traced here: 20.4 us
  Pallas kernels  19.8 us (96%)
  between operations  0.66 us (3%)
    pallas_call x1, Pallas kernels, per_device(): pl.pallas_call(functools.partial(gather_kernel, nf, nc, img, band, lean,...  18.2 us
    pallas_call x1, Pallas kernels, per_device(): pl.pallas_call(v_kernel, out_shape=jax.ShapeDtypeStruct((SG, 2 * SG), F32...  1.59 us

profile of v4, /device:TPU:0, one launch (start us, length us, event | category | flops | bytes accessed | tf_op | source)
XLA Modules:
  0.0 20.4 jit_solution(12797420410224257942)
XLA Ops:
  0.7 18.2 %gather_columns.1 = (f32[512,1024]{1,0:T(8,128)S(1)}, f32[32,1024]{1,0:T(8,128)S(1)}, bf16[512,256]{1,0:T(8,128)(2,1)S(1)}) custom-call(s32[1]{0:T(128)S(6)} %copy.7.fx_ref, s32[2]{0:T(128)} %fy_hbm.1, s32[8]{0:T(128)} %u_hbm.1, s32[8]{0:T(128)} %bitcast.5, s32[8]{0:T(128)} %bitcast.6, f32[48,2,1024]{2,1,0:T(2,128)} %bitcast.4), custom_call_target="tpu_custom_call" | custom-call | tf_op jit(solution)/shard_map/gather_columns/pallas_call | solution.py:452
  18.9 1.6 %v_transform.1 = f32[512,1024]{1,0:T(8,128)} custom-call(f32[512,1024]{1,0:T(8,128)S(1)} %get-tuple-element.8.acc_ref, f32[32,1024]{1,0:T(8,128)S(1)} %get-tuple-element.9.h_ref, bf16[512,256]{1,0:T(8,128)(2,1)S(1)} %get-tuple-element.10.e_ref), custom_call_target="tpu_custom_call" | custom-call | tf_op jit(solution)/shard_map/v_transform/pallas_call | solution.py:490

commit v5 on v4

--- a/solution.py
+++ b/solution.py
@@ -446,7 +446,7 @@
     half = width // 2
     tail = (rpd - rpd // 3) * nf
     lean = rpd // 6
-    tilt = 1
+    tilt = 2 * (rpd // 6)
     vm = pl.BlockSpec(memory_space=pltpu.VMEM)
     dma = pltpu.SemaphoreType.DMA
     acc, h, e = pl.pallas_call(

time: 20.6 us -> 20.5 us (level)
  no operation moved by 1% of the time
where the time goes in v5:
time: 20.5 us; the launch traced here: 20.3 us
  Pallas kernels  19.7 us (96%)
  between operations  0.66 us (3%)
    pallas_call x1, Pallas kernels, per_device(): pl.pallas_call(functools.partial(gather_kernel, nf, nc, img, band, lean,...  18.1 us
    pallas_call x1, Pallas kernels, per_device(): pl.pallas_call(v_kernel, out_shape=jax.ShapeDtypeStruct((SG, 2 * SG), F32...  1.59 us

profile of v5, /device:TPU:0, one launch (start us, length us, event | category | flops | bytes accessed | tf_op | source)
XLA Modules:
  0.0 20.3 jit_solution(9150107287868109064)
XLA Ops:
  0.7 18.1 %gather_columns.1 = (f32[512,1024]{1,0:T(8,128)S(1)}, f32[32,1024]{1,0:T(8,128)S(1)}, bf16[512,256]{1,0:T(8,128)(2,1)S(1)}) custom-call(s32[1]{0:T(128)S(6)} %copy.7.fx_ref, s32[2]{0:T(128)} %fy_hbm.1, s32[8]{0:T(128)} %u_hbm.1, s32[8]{0:T(128)} %bitcast.5, s32[8]{0:T(128)} %bitcast.6, f32[48,2,1024]{2,1,0:T(2,128)} %bitcast.4), custom_call_target="tpu_custom_call" | custom-call | tf_op jit(solution)/shard_map/gather_columns/pallas_call | solution.py:452
  18.7 1.6 %v_transform.1 = f32[512,1024]{1,0:T(8,128)} custom-call(f32[512,1024]{1,0:T(8,128)S(1)} %get-tuple-element.8.acc_ref, f32[32,1024]{1,0:T(8,128)S(1)} %get-tuple-element.9.h_ref, bf16[512,256]{1,0:T(8,128)(2,1)S(1)} %get-tuple-element.10.e_ref), custom_call_target="tpu_custom_call" | custom-call | tf_op jit(solution)/shard_map/v_transform/pallas_call | solution.py:490

commit v6 on v5

--- a/solution.py
+++ b/solution.py
@@ -176,12 +176,13 @@
     def keep(row, slot):
         pltpu.make_async_copy(vfac.at[row], cells.at[slot, :, f], r_a2a.at[slot]).start()
 
+    even = f - lax.rem(f, 2)
+    peers = [partner(even, nf, d) for d in far_first(nf) if d > 1] + [partner(f, nf, 1)]
     for y in range(most - 1):
         if y < 2:
             done(vfac.at[pl.ds(0, nf if y == 0 else rows - nf)], f_sem.at[y])
         sure = y < least - 1
-        for d in far_first(nf):
-            peer = partner(f, nf, d)
+        for peer in peers:
             if sure:
                 send(first_row(peer) + y, peer, c, y)
             else:
@@ -224,8 +225,7 @@
     lax.fori_loop(0, half // block, table_step, 0)
 
     plane = jnp.where(c > 0, c - 1, 0)
-    for d in far_first(nf):
-        peer = partner(f, nf, d)
+    for peer in peers:
         last = count_of(peer) - 1
         send(first_row(peer) + last, peer, plane, jnp.where(c > 0, most, last))
     pl.when(c > 0)(functools.partial(send, start + count - 1, f, plane, most))

time: 20.5 us -> 20.5 us (level)
  no operation moved by 1% of the time
where the time goes in v6:
time: 20.5 us; the launch traced here: 20.3 us
  Pallas kernels  19.7 us (96%)
  between operations  0.66 us (3%)
    pallas_call x1, Pallas kernels, per_device(): pl.pallas_call(functools.partial(gather_kernel, nf, nc, img, band, lean,...  18.1 us
    pallas_call x1, Pallas kernels, per_device(): pl.pallas_call(v_kernel, out_shape=jax.ShapeDtypeStruct((SG, 2 * SG), F32...  1.59 us

profile of v6, /device:TPU:0, one launch (start us, length us, event | category | flops | bytes accessed | tf_op | source)
XLA Modules:
  0.0 20.3 jit_solution(278070460839994888)
XLA Ops:
  0.7 18.1 %gather_columns.1 = (f32[512,1024]{1,0:T(8,128)S(1)}, f32[32,1024]{1,0:T(8,128)S(1)}, bf16[512,256]{1,0:T(8,128)(2,1)S(1)}) custom-call(s32[1]{0:T(128)S(6)} %copy.7.fx_ref, s32[2]{0:T(128)} %fy_hbm.1, s32[8]{0:T(128)} %u_hbm.1, s32[8]{0:T(128)} %bitcast.5, s32[8]{0:T(128)} %bitcast.6, f32[48,2,1024]{2,1,0:T(2,128)} %bitcast.4), custom_call_target="tpu_custom_call" | custom-call | tf_op jit(solution)/shard_map/gather_columns/pallas_call | solution.py:452
  18.7 1.6 %v_transform.1 = f32[512,1024]{1,0:T(8,128)} custom-call(f32[512,1024]{1,0:T(8,128)S(1)} %get-tuple-element.8.acc_ref, f32[32,1024]{1,0:T(8,128)S(1)} %get-tuple-element.9.h_ref, bf16[512,256]{1,0:T(8,128)(2,1)S(1)} %get-tuple-element.10.e_ref), custom_call_target="tpu_custom_call" | custom-call | tf_op jit(solution)/shard_map/v_transform/pallas_call | solution.py:490

commit v7 on v6

--- a/solution.py
+++ b/solution.py
@@ -92,7 +92,7 @@
     acc_ref, h_ref, e_ref,
     vfac, f_sem, hbuf, e1, rhs, cells, fxs, fxall, table, premod, phase, eo, zbuf, part, zrecv, gsend,
     fy_ref, u_ref, sc_ref, sv_ref,
-    s_a2a, r_a2a, x_sem, s_z, r_z, g_sem, i_sem, z_sem,
+    s_out, r_a2a, x_sem, r_z, g_sem, i_sem, z_sem,
 ):
     f = lax.axis_index("facet")
     c = lax.axis_index("col")
@@ -161,15 +161,15 @@
 
     for d in far_first(nf):
         pltpu.make_async_remote_copy(
-            src_ref=fxs, dst_ref=fxall.at[f], send_sem=x_sem.at[0], recv_sem=x_sem.at[1],
+            src_ref=fxs, dst_ref=fxall.at[f], send_sem=s_out, recv_sem=x_sem,
             device_id=(partner(f, nf, d), c), device_id_type=MESH,
         ).start()
-    pltpu.make_async_copy(fxs, fxall.at[f], x_sem.at[1]).start()
+    pltpu.make_async_copy(fxs, fxall.at[f], x_sem).start()
 
     def send(row, peer, plane, slot):
         pltpu.make_async_remote_copy(
             src_ref=vfac.at[row], dst_ref=cells.at[slot, :, f],
-            send_sem=s_a2a, recv_sem=r_a2a.at[slot],
+            send_sem=s_out, recv_sem=r_a2a.at[slot],
             device_id=(peer, plane), device_id_type=MESH,
         ).start()
 
@@ -265,7 +265,7 @@
         lax.fori_loop(0, SG // block, v_step, 0)
 
     part[...] = jnp.zeros_like(part)
-    done(fxall, x_sem.at[1])
+    done(fxall, x_sem)
     lane = lax.broadcasted_iota(I32, (ncol, SG), 1)
     uv = jnp.zeros((ncol, SG), I32)
     row = lax.broadcasted_iota(I32, (ncol, SG), 0)
@@ -344,7 +344,7 @@
                 owner = jnp.where(d < c, d, d + 1)
                 pltpu.make_async_remote_copy(
                     src_ref=part.at[y, pl.ds(owner * COLS_DEV, COLS_DEV)], dst_ref=zrecv.at[y, c],
-                    send_sem=s_z, recv_sem=r_z.at[y],
+                    send_sem=s_out, recv_sem=r_z.at[y],
                     device_id=(f, owner), device_id_type=MESH,
                 ).start()
             pltpu.make_async_copy(
@@ -367,7 +367,7 @@
     def sum_step(early, planes, y, carry):
         target = hbuf if early else h_ref
         place = y * nf + f if early else tail_row + y - cut
-        sem = g_sem.at[1 if early else 2]
+        sem = g_sem.at[0 if early else 1]
         done(zrecv.at[y, pl.ds(0, planes)], r_z.at[y])
         acc = zrecv[y, 0]
         for d in range(1, planes):
@@ -384,7 +384,7 @@
             peer = jnp.where(i < f, i, i + 1)
             pltpu.make_async_remote_copy(
                 src_ref=gsend.at[y, peer], dst_ref=target.at[place],
-                send_sem=g_sem.at[0], recv_sem=sem,
+                send_sem=s_out, recv_sem=sem,
                 device_id=(peer, c), device_id_type=MESH,
             ).start()
         pltpu.make_async_copy(gsend.at[y, f], target.at[place], sem).start()
@@ -408,15 +408,15 @@
 
         lax.fori_loop(0, times, step, 0)
 
-    done(fxall.at[pl.ds(0, nf - 1)], x_sem.at[0])
-    done(facets_ref.at[pl.ds(0, rows - most)], s_a2a)
-    drain(facets_ref.at[pl.ds(0, 1)], s_a2a, most - own)
-    drain(zrecv.at[0, pl.ds(1, nc - 1)], s_z, count - jnp.where(c < nc - 1, 0, 1))
-    done(hbuf, g_sem.at[1])
+    done(fxall.at[pl.ds(0, nf - 1)], s_out)
+    done(facets_ref.at[pl.ds(0, rows - most)], s_out)
+    drain(facets_ref.at[pl.ds(0, 1)], s_out, most - own)
+    drain(zrecv.at[0, pl.ds(1, nc - 1)], s_out, count - jnp.where(c < nc - 1, 0, 1))
+    done(hbuf, g_sem.at[0])
     stack(hbuf, rhs)
     acc_ref[...] = mm(e1[...], rhs[...])
-    drain(facets_ref.at[pl.ds(0, (nf - 1) * 2 * SG // width), 0], g_sem.at[0], count)
-    done(h_ref, g_sem.at[2])
+    drain(facets_ref.at[pl.ds(0, (nf - 1) * 2 * SG // width), 0], s_out, count)
+    done(h_ref, g_sem.at[1])
 
 
 def v_kernel(acc_ref, h_ref, e_ref, out_ref, rhs, buf, sem):
@@ -476,7 +476,7 @@
             pltpu.VMEM((rpd + lean + tilt, nf, 2 * SG), F32),
             pltpu.SMEM((2,), I32), pltpu.SMEM((ncol,), I32),
             pltpu.SMEM((nf,), I32), pltpu.SMEM((nf,), I32),
-            dma(()), dma((rpd + lean + tilt + 1,)), dma((2,)), dma(()), dma((rpd + lean + tilt,)), dma((3,)), dma((4,)),
+            dma(()), dma((rpd + lean + tilt + 1,)), dma(()), dma((rpd + lean + tilt,)), dma((2,)), dma((4,)),
             pltpu.SemaphoreType.REGULAR,
         ],
         compiler_params=pltpu.CompilerParams(

time: 20.5 us -> 20.4 us (level)
  no operation moved by 1% of the time
where the time goes in v7:
time: 20.4 us; the launch traced here: 20.3 us
  Pallas kernels  19.6 us (96%)
  between operations  0.66 us (3%)
    pallas_call x1, Pallas kernels, per_device(): pl.pallas_call(functools.partial(gather_kernel, nf, nc, img, band, lean,...  18 us
    pallas_call x1, Pallas kernels, per_device(): pl.pallas_call(v_kernel, out_shape=jax.ShapeDtypeStruct((SG, 2 * SG), F32...  1.59 us

profile of v7, /device:TPU:0, one launch (start us, length us, event | category | flops | bytes accessed | tf_op | source)
XLA Modules:
  0.0 20.3 jit_solution(8545672340547409631)
XLA Ops:
  0.7 18.0 %gather_columns.1 = (f32[512,1024]{1,0:T(8,128)S(1)}, f32[32,1024]{1,0:T(8,128)S(1)}, bf16[512,256]{1,0:T(8,128)(2,1)S(1)}) custom-call(s32[1]{0:T(128)S(6)} %copy.7.fx_ref, s32[2]{0:T(128)} %fy_hbm.1, s32[8]{0:T(128)} %u_hbm.1, s32[8]{0:T(128)} %bitcast.5, s32[8]{0:T(128)} %bitcast.6, f32[48,2,1024]{2,1,0:T(2,128)} %bitcast.4), custom_call_target="tpu_custom_call" | custom-call | tf_op jit(solution)/shard_map/gather_columns/pallas_call | solution.py:452
  18.7 1.6 %v_transform.1 = f32[512,1024]{1,0:T(8,128)} custom-call(f32[512,1024]{1,0:T(8,128)S(1)} %get-tuple-element.8.acc_ref, f32[32,1024]{1,0:T(8,128)S(1)} %get-tuple-element.9.h_ref, bf16[512,256]{1,0:T(8,128)(2,1)S(1)} %get-tuple-element.10.e_ref), custom_call_target="tpu_custom_call" | custom-call | tf_op jit(solution)/shard_map/v_transform/pallas_call | solution.py:490
